TPU v7x, 32 devices: a whole 2x2x4 slice. The times are simulated.
32 devices in a mesh: group: 8 (over y, x, core), member: 4 (over z).
Axes of the slice: x: 2, y: 2, z: 4, core: 2. Of those that a mesh axis runs over, the one named last changes fastest.
Arguments:
- tokens: bfloat16 [4096, 2048], P(('group', 'member')), may hold values from -6 to 6
- grad_out: bfloat16 [4096, 2048], P(('group', 'member')), may hold values from -6 to 6
- expert_ids: int32 [4096, 8], P(('group', 'member')), may hold values from 0 to 31, as said below
- pair_slot: int32 [4096, 8], P(('group', 'member')), may hold values from 0 to 47, as said below
- gate_weights: bfloat16 [4096, 8], P(('group', 'member')), may hold values from 0.049804688 to 1
- weight_gate: bfloat16 [32, 2048, 768], P(('group', 'member')), may hold values from -0.125 to 0.125
- weight_up: bfloat16 [32, 2048, 768], P(('group', 'member')), may hold values from -0.125 to 0.125
- weight_down: bfloat16 [32, 768, 2048], P(('group', 'member')), may hold values from -0.21875 to 0.21875
- saved_gate: bfloat16 [32, 1536, 768], P(('group', 'member')), may hold values from -6 to 6
- saved_up: bfloat16 [32, 1536, 768], P(('group', 'member')), may hold values from -6 to 6
Outputs:
- grad_tokens: bfloat16 [4096, 2048], P(('group', 'member'))
- grad_gates: bfloat16 [4096, 8], P(('group', 'member'))
- grad_weight_gate: bfloat16 [32, 2048, 768], P(('group', 'member'))
- grad_weight_up: bfloat16 [32, 2048, 768], P(('group', 'member'))
- grad_weight_down: bfloat16 [32, 768, 2048], P(('group', 'member'))
Inputs may be any that keep to these rules, and one draw needn't show every extreme that they name: `expert_ids`: each token names 8 distinct experts, two in each of exactly 4 groups, the group of expert e being e // 4. The tokens of one device send at most 96 tokens to one group, and in every draw some group gets exactly 96 from every device. `pair_slot`: among one device's assignments to one expert the slots are distinct and run from 0 to their count less one, in no fixed order of tokens. In every draw some expert gets exactly 48 assignments from every device.
All inputs are finite; a program needn't handle non-finite values.
Results may differ from a plain program's by a relative error of at most 0.012.
Values may be sent and summed in bfloat16 or wider, within the bound.
A program may use at most 192 MiB of HBM per device.

v0:
```python
import jax
import jax.numpy as jnp
from jax import lax
from jax.sharding import PartitionSpec as P


def expert_block(
    token_rows,
    grad_rows,
    route_gate,
    saved_pregate,
    saved_preup,
    weight_gate,
    weight_up,
    weight_down,
):
    pre_gate = saved_pregate.astype(jnp.float32)
    pre_up = saved_preup.astype(jnp.float32)
    gate_sigmoid = jax.nn.sigmoid(pre_gate)
    gate_swish = pre_gate * gate_sigmoid
    hidden = gate_swish * pre_up
    hidden_low = hidden.astype(jnp.bfloat16)
    route_scale = route_gate.astype(jnp.float32)[:, None]
    scaled_grads = (route_scale * grad_rows.astype(jnp.float32)).astype(jnp.bfloat16)
    over_rows = (((0,), (0,)), ((), ()))
    over_features = (((1,), (1,)), ((), ()))
    down_grad = lax.dot_general(
        hidden_low, scaled_grads, over_rows, preferred_element_type=jnp.float32
    )
    back_hidden = lax.dot_general(
        grad_rows, weight_down, over_features, preferred_element_type=jnp.float32
    )
    slot_gate = jnp.sum(hidden * back_hidden, axis=1).astype(jnp.bfloat16)
    hidden_grad = route_scale * back_hidden
    pregate_grad = (
        hidden_grad * pre_up * gate_sigmoid * (1.0 + pre_gate * (1.0 - gate_sigmoid))
    ).astype(jnp.bfloat16)
    preup_grad = (hidden_grad * gate_swish).astype(jnp.bfloat16)
    gate_grad = lax.dot_general(
        token_rows, pregate_grad, over_rows, preferred_element_type=jnp.float32
    )
    up_grad = lax.dot_general(token_rows, preup_grad, over_rows, preferred_element_type=jnp.float32)
    slot_grad = (
        lax.dot_general(
            pregate_grad, weight_gate, over_features, preferred_element_type=jnp.float32
        )
        + lax.dot_general(preup_grad, weight_up, over_features, preferred_element_type=jnp.float32)
    ).astype(jnp.bfloat16)
    return (slot_grad, slot_gate, gate_grad, up_grad, down_grad)


def body(
    tokens,
    grad_out,
    expert_ids,
    pair_slot,
    gate_weights,
    weight_gate,
    weight_up,
    weight_down,
    saved_gate,
    saved_up,
):
    groups = lax.axis_size("group")
    members = lax.axis_size("member")
    experts = groups * members
    tok_rows, model_width = tokens.shape
    route_count = expert_ids.shape[1]
    capacity = saved_gate.shape[1]
    pair_rows = capacity // experts
    token_range = jnp.arange(tok_rows, dtype=jnp.int32)
    dest = (expert_ids * pair_rows + pair_slot).reshape(-1)
    slot_token = (
        jnp.full((experts * pair_rows,), tok_rows, jnp.int32)
        .at[dest]
        .set(jnp.repeat(token_range, route_count))
    )
    send_rows = jnp.take(tokens, slot_token, axis=0, mode="fill", fill_value=0)
    send_grads = jnp.take(grad_out, slot_token, axis=0, mode="fill", fill_value=0)
    send_gates = (
        jnp.zeros((experts * pair_rows,), jnp.bfloat16).at[dest].set(gate_weights.reshape(-1))
    )
    expert_rows, expert_grads, expert_gates = (
        lax.all_to_all(send_rows, ("group", "member"), split_axis=0, concat_axis=0, tiled=True),
        lax.all_to_all(send_grads, ("group", "member"), split_axis=0, concat_axis=0, tiled=True),
        lax.all_to_all(send_gates, ("group", "member"), split_axis=0, concat_axis=0, tiled=True),
    )
    slot_grad, slot_gate, gate_total, up_total, down_total = expert_block(
        expert_rows,
        expert_grads,
        expert_gates,
        saved_gate[0],
        saved_up[0],
        weight_gate[0],
        weight_up[0],
        weight_down[0],
    )
    back_rows, back_terms = (
        lax.all_to_all(slot_grad, ("group", "member"), split_axis=0, concat_axis=0, tiled=True),
        lax.all_to_all(slot_gate, ("group", "member"), split_axis=0, concat_axis=0, tiled=True),
    )
    per_route = jnp.take(back_rows, dest, axis=0).reshape(tok_rows, route_count, model_width)
    grad_tokens = jnp.sum(per_route.astype(jnp.float32), axis=1).astype(jnp.bfloat16)
    grad_gates = jnp.take(back_terms, dest, axis=0).reshape(tok_rows, route_count)
    return (
        grad_tokens,
        grad_gates,
        gate_total[None].astype(jnp.bfloat16),
        up_total[None].astype(jnp.bfloat16),
        down_total[None].astype(jnp.bfloat16),
    )


def solution(mesh):
    return jax.shard_map(
        body,
        mesh=mesh,
        in_specs=(
            P(("group", "member"), None),
            P(("group", "member"), None),
            P(("group", "member"), None),
            P(("group", "member"), None),
            P(("group", "member"), None),
            P(("group", "member"), None, None),
            P(("group", "member"), None, None),
            P(("group", "member"), None, None),
            P(("group", "member"), None, None),
            P(("group", "member"), None, None),
        ),
        out_specs=(
            P(("group", "member"), None),
            P(("group", "member"), None),
            P(("group", "member"), None, None),
            P(("group", "member"), None, None),
            P(("group", "member"), None, None),
        ),
        check_vma=False,
    )
```

profile of v0, /device:TPU:9, one launch (start us, length us, event | category | flops | bytes accessed | tf_op | source)
XLA Modules:
  0.0 526.1 jit_solution(164562047972256510)
XLA Ops:
  0.6 0.0 copy-start
  0.6 0.9 copy.44
  1.6 0.1 reshape.154
  1.7 0.7 multiply_add_fusion
  2.4 0.1 copy.43
  2.5 0.1 reshape.111
  2.6 7.6 %scatter_custom_fusion = bf16[1536]{0:T(1024)(128)(2,1)S(1)} fusion(s32[1024]{0:T(1024)S(1)} %bitcast.91, bf16[1024]{0:T(1024)(128)(2,1)S(1)} %reshape.154, bf16[]{:T(256)} %constant.33.clone.1), kind=kCustom, calls=%fused_computation.58 | custom fusion | bytes 3074 | tf_op jit(solution)/shard_map/scatter | solution.py:81
  10.2 0.7 all_to_all.49
  10.9 6.3 %all-to-all-start = ((bf16[32,48,1]{1,2,0:T(2,128)(2,1)}), bf16[32,48,1]{1,2,0:T(2,128)(2,1)S(1)}, u32[]{:S(2)}, u32[]{:S(2)}) async-start(bf16[32,48,1]{1,2,0:T(2,128)(2,1)} %all_to_all.49), calls=%async_computation | async-start | bytes 32768 | tf_op jit(solution)/shard_map/all_to_all | solution.py:86
  17.3 0.1 reshape.162
  17.4 4.3 scatter_custom_fusion.1
  21.7 13.8 %gather_fusion.3 = bf16[1536,2048]{1,0:T(8,128)(2,1)} fusion(bf16[128,2048]{1,0:T(8,128)(2,1)} %param.12, s32[2048]{0:T(1024)S(1)} %pad_clamp_fusion), kind=kCustom, calls=%fused_computation.1.clone | custom fusion | bytes 12589056 | tf_op jit(solution)/shard_map/jit(_take)/gather | solution.py:78
  35.6 13.8 %gather_fusion.2 = bf16[1536,2048]{1,0:T(8,128)(2,1)} fusion(bf16[128,2048]{1,0:T(8,128)(2,1)} %param.13, s32[2048]{0:T(1024)S(1)} %pad_clamp_fusion), kind=kCustom, calls=%fused_computation.clone | custom fusion | bytes 12589056 | tf_op jit(solution)/shard_map/jit(_take)/gather | solution.py:79
  49.3 10.5 %broadcast_select_fusion = (bf16[1536,2048]{1,0:T(8,128)(2,1)}, bf16[1536,2048]{1,0:T(8,128)(2,1)}) fusion(bf16[1536,2048]{1,0:T(8,128)(2,1)} %gather_fusion.3, pred[1536]{0:T(1024)(128)(4,1)S(1)} %compare_and_fusion, bf16[1536,2048]{1,0:T(8,128)(2,1)} %gather_fusion.2), kind=kLoop, calls=%fused_computation.14 | loop fusion | flops 6291456 | bytes 25167360 | tf_op jit(solution)/shard_map/jit(_take)/select_n | solution.py:78
  59.8 0.0 all-to-all-done
  59.8 143.0 %all_to_all.55 = bf16[32,48,2048]{2,1,0:T(8,128)(2,1)} all-to-all(bf16[32,48,2048]{2,1,0:T(8,128)(2,1)} %bitcast.87), channel_id=1, replica_groups=mesh['group'=8,'member'=4] {'group','member'}, dimensions={0} | all-to-all | bytes 12582912 | tf_op jit(solution)/shard_map/all_to_all | solution.py:85
  202.8 4.8 all-to-all-start.4
  207.7 4.3 copy.47
  212.0 4.3 copy.46
  216.2 0.1 convert_reduce_fusion
  216.3 0.1 reshape.114
  216.4 12.7 %fusion.9 = (bf16[1536]{0:T(1024)(128)(2,1)S(1)}, bf16[1536,768]{0,1:T(8,128)(2,1)}, bf16[1536,768]{0,1:T(8,128)(2,1)}) fusion(bf16[1,1536,768]{1,2,0:T(8,128)(2,1)} %copy.46, bf16[1,1536,768]{1,2,0:T(8,128)(2,1)} %copy.47, f32[1536]{0:T(1024)S(1)} %reshape.114, bf16[1536,2048]{1,0:T(8,128)(2,1)} %bitcast.85, bf16[1,768,2048]{2,1,0:T(8,128)(2,1)} %param.19), kind=kOutput, calls=%fused_computation.24 | convolution fusion | flops 4854249984 | bytes 18883584 | tf_op jit(solution)/shard_map/dot_general | solution.py:30
  229.0 0.7 convert_element_type.122
  229.7 0.0 copy-done
  229.7 9.6 %fusion.20 = f32[1536,2048]{1,0:T(8,128)} fusion(bf16[1536,768]{0,1:T(8,128)(2,1)} %get-tuple-element.24, bf16[1,2048,768]{2,1,0:T(8,128)(2,1)S(1)} %copy-done), kind=kOutput, calls=%fused_computation.40 | convolution fusion | flops 4831838208 | bytes 18087936 | tf_op jit(solution)/shard_map/dot_general | solution.py:44
  239.3 108.4 %all-to-all-done.4 = bf16[32,48,2048]{2,1,0:T(8,128)(2,1)} async-done(((bf16[32,48,2048]{2,1,0:T(8,128)(2,1)}), bf16[32,48,2048]{2,1,0:T(8,128)(2,1)}, u32[]{:S(2)}, u32[]{:S(2)}) %all-to-all-start.4) | async-done | bytes 6291488 | tf_op jit(solution)/shard_map/all_to_all | solution.py:84
  347.7 3.7 all-to-all-start.3
  351.4 11.1 %add_convert_fusion = bf16[1536,2048]{1,0:T(8,128)(2,1)} fusion(f32[1536,2048]{1,0:T(8,128)} %fusion.20, bf16[1536,768]{0,1:T(8,128)(2,1)} %get-tuple-element.25, bf16[1,2048,768]{2,1,0:T(8,128)(2,1)} %param.18), kind=kOutput, calls=%fused_computation.7 | convolution fusion | flops 4838129664 | bytes 24379392 | tf_op jit(solution)/shard_map/dot_general | solution.py:47
  362.5 0.0 all-to-all-done.3
  362.5 5.9 %all-to-all-start.2 = ((bf16[32,48,2048]{2,1,0:T(8,128)(2,1)}), bf16[32,48,2048]{2,1,0:T(8,128)(2,1)}, u32[]{:S(2)}, u32[]{:S(2)}) async-start(bf16[32,48,2048]{2,1,0:T(8,128)(2,1)} %bitcast.88), calls=%async_computation.2 | async-start | bytes 12582912 | tf_op jit(solution)/shard_map/all_to_all | solution.py:99
  368.4 0.0 copy-start.4
  368.4 4.0 multiply_convert_fusion
  372.5 0.0 copy-done.4
  372.5 0.0 copy-start.5
  372.5 9.7 %fusion.24 = bf16[1,2048,768]{2,1,0:T(8,128)(2,1)} fusion(bf16[1536,2048]{1,0:T(8,128)(2,1)} %bitcast.12, bf16[1536,768]{0,1:T(8,128)(2,1)S(1)} %copy-done.4), kind=kOutput, calls=%fused_computation.44 | convolution fusion | flops 4833411072 | bytes 11796480 | tf_op jit(solution)/shard_map/dot_general | solution.py:39
  382.2 0.0 copy-done.5
  382.2 0.0 copy-start.2
  382.2 0.0 copy-start.3
  382.2 9.8 %fusion.25 = bf16[1,2048,768]{2,1,0:T(8,128)(2,1)} fusion(bf16[1536,2048]{1,0:T(8,128)(2,1)} %bitcast.12, bf16[1536,768]{0,1:T(8,128)(2,1)S(1)} %copy-done.5), kind=kOutput, calls=%fused_computation.45 | convolution fusion | flops 4833411072 | bytes 11796480 | tf_op jit(solution)/shard_map/dot_general | solution.py:42
  392.0 0.0 copy-done.2
  392.0 0.0 copy-done.3
  392.0 6.9 %fusion.26 = bf16[1,768,2048]{2,1,0:T(8,128)(2,1)} fusion(bf16[1536,2048]{1,0:T(8,128)(2,1)S(1)} %bitcast.89, bf16[1,1536,768]{1,2,0:T(8,128)(2,1)S(1)} %copy-done.3, bf16[1,1536,768]{1,2,0:T(8,128)(2,1)S(1)} %copy-done.2), kind=kOutput, calls=%fused_computation.46 | convolution fusion | flops 4842848256 | bytes 14155776 | tf_op jit(solution)/shard_map/dot_general | solution.py:27
  398.9 0.1 reduce.2
  399.0 0.1 all_to_all.45
  399.0 6.8 %gather_fusion.1 = bf16[1024]{0:T(1024)(128)(2,1)S(1)} fusion(bf16[1536]{0:T(1024)(128)(2,1)S(1)} %all_to_all.45, s32[1024]{0:T(1024)S(1)} %broadcast_clamp_fusion), kind=kCustom, calls=%fused_computation.3 | custom fusion | bytes 8192 | tf_op jit(solution)/shard_map/jit(_take)/gather | solution.py:104
  405.8 0.1 gather.18
  405.9 0.1 copy.49
  406.0 0.6 broadcast_select_fusion.2
  406.6 0.1 copy.42
  406.7 101.7 %all-to-all-done.2 = bf16[32,48,2048]{2,1,0:T(8,128)(2,1)} async-done(((bf16[32,48,2048]{2,1,0:T(8,128)(2,1)}), bf16[32,48,2048]{2,1,0:T(8,128)(2,1)}, u32[]{:S(2)}, u32[]{:S(2)}) %all-to-all-start.2) | async-done | bytes 6291488 | tf_op jit(solution)/shard_map/all_to_all | solution.py:99
  508.4 0.0 copy-start.1
  508.4 12.5 %gather_fusion = bf16[1024,2048]{1,0:T(8,128)(2,1)} fusion(bf16[1536,2048]{1,0:T(8,128)(2,1)} %bitcast.9, s32[1024]{0:T(1024)S(1)} %broadcast_clamp_fusion), kind=kCustom, calls=%fused_computation.2 | custom fusion | bytes 8392704 | tf_op jit(solution)/shard_map/jit(_take)/gather | solution.py:102
  521.0 5.1 fusion.18
  526.1 0.0 copy-done.1
  (7 shorter events, 0.1 us)
Async XLA Ops:
  0.6 229.1 %copy-start = (bf16[1,2048,768]{2,1,0:T(8,128)(2,1)S(1)}, bf16[1,2048,768]{2,1,0:T(8,128)(2,1)}, u32[]{:S(2)}) copy-start(bf16[1,2048,768]{2,1,0:T(8,128)(2,1)} %param.17) | copy-start | bytes 9437188
  10.9 48.9 %all-to-all-start = ((bf16[32,48,1]{1,2,0:T(2,128)(2,1)}), bf16[32,48,1]{1,2,0:T(2,128)(2,1)S(1)}, u32[]{:S(2)}, u32[]{:S(2)}) async-start(bf16[32,48,1]{1,2,0:T(2,128)(2,1)} %all_to_all.49), calls=%async_computation | async-start | bytes 32768 | tf_op jit(solution)/shard_map/all_to_all | solution.py:86
  202.8 144.9 %all-to-all-start.4 = ((bf16[32,48,2048]{2,1,0:T(8,128)(2,1)}), bf16[32,48,2048]{2,1,0:T(8,128)(2,1)}, u32[]{:S(2)}, u32[]{:S(2)}) async-start(bf16[32,48,2048]{2,1,0:T(8,128)(2,1)} %bitcast.86), calls=%async_computation.4 | async-start | bytes 12582912 | tf_op jit(solution)/shard_map/all_to_all | solution.py:84
  347.7 14.8 %all-to-all-start.3 = ((bf16[32,48,1]{1,2,0:T(2,128)(2,1)}), bf16[32,48,1]{1,2,0:T(2,128)(2,1)S(1)}, u32[]{:S(2)}, u32[]{:S(2)}) async-start(bf16[32,48,1]{1,2,0:T(2,128)(2,1)} %convert_element_type.122), calls=%async_computation.3 | async-start | bytes 32768 | tf_op jit(solution)/shard_map/all_to_all | solution.py:100
  362.5 146.0 %all-to-all-start.2 = ((bf16[32,48,2048]{2,1,0:T(8,128)(2,1)}), bf16[32,48,2048]{2,1,0:T(8,128)(2,1)}, u32[]{:S(2)}, u32[]{:S(2)}) async-start(bf16[32,48,2048]{2,1,0:T(8,128)(2,1)} %bitcast.88), calls=%async_computation.2 | async-start | bytes 12582912 | tf_op jit(solution)/shard_map/all_to_all | solution.py:99
  368.4 4.0 copy-start.4
  372.5 9.7 %copy-start.5 = (bf16[1536,768]{0,1:T(8,128)(2,1)S(1)}, bf16[1536,768]{0,1:T(8,128)(2,1)}, u32[]{:S(2)}) copy-start(bf16[1536,768]{0,1:T(8,128)(2,1)} %get-tuple-element.25) | copy-start | bytes 7077892
  382.2 9.8 %copy-start.2 = (bf16[1,1536,768]{1,2,0:T(8,128)(2,1)S(1)}, bf16[1,1536,768]{1,2,0:T(8,128)(2,1)}, u32[]{:S(2)}) copy-start(bf16[1,1536,768]{1,2,0:T(8,128)(2,1)} %copy.47) | copy-start | bytes 7077892
  382.2 9.8 %copy-start.3 = (bf16[1,1536,768]{1,2,0:T(8,128)(2,1)S(1)}, bf16[1,1536,768]{1,2,0:T(8,128)(2,1)}, u32[]{:S(2)}) copy-start(bf16[1,1536,768]{1,2,0:T(8,128)(2,1)} %copy.46) | copy-start | bytes 7077892
  508.4 17.7 %copy-start.1 = (bf16[1,2048,768]{2,1,0:T(8,128)(2,1)S(1)}, bf16[1,2048,768]{2,1,0:T(8,128)(2,1)}, u32[]{:S(2)}) copy-start(bf16[1,2048,768]{2,1,0:T(8,128)(2,1)} %param.17) | copy-start | bytes 9437188
where the time goes:
time: 527 us; the launch traced here: 526 us
  waiting for transfers between devices  210 us (40%)
  blocking collectives  143 us (27%)
  local copies, waits for them, and re-layouts  70.7 us (13%)
  matrix products  59.7 us (11%)
  other arithmetic  21.1 us (4%)
  starting transfers between devices  20.7 us (4%)
    all_to_all x1, blocking collectives, body(): lax.all_to_all(send_grads, ('group', 'member'), split_axis=0, concat_axis...  143 us
    all_to_all x1, waiting for transfers between devices, body(): lax.all_to_all(send_rows, ('group', 'member'), split_axis=0, concat_axis=...  108 us
    all_to_all x1, waiting for transfers between devices, body(): lax.all_to_all(slot_grad, ('group', 'member'), split_axis=0, concat_axis=...  102 us
    gather x1, local copies, waits for them, and re-layouts, body(): send_rows = jnp.take(tokens, slot_token, axis=0, mode='fill', fill_value=0)  13.8 us
    gather x1, local copies, waits for them, and re-layouts, body(): jnp.take(grad_out, slot_token, axis=0, mode='fill', fill_value=0)  13.8 us
    dot_general x1, matrix products, expert_block(): lax.dot_general(grad_rows, weight_down, over_features, preferred_element_...  12.7 us
    gather x1, local copies, waits for them, and re-layouts, body(): jnp.take(back_rows, dest, axis=0)  12.5 us
    dot_general x1, matrix products, expert_block(): lax.dot_general(preup_grad, weight_up, over_features, preferred_element_t...  11.1 us
  transfers between devices with their start and end apart: 4, of which 2 were waited for; matrix products, arithmetic and copies ran while one was open for 23% of the time, Pallas kernels for 0%

commit v1 on v0

--- a/solution.py
+++ b/solution.py
@@ -2,6 +2,10 @@
 import jax.numpy as jnp
 from jax import lax
 from jax.sharding import PartitionSpec as P
+
+AXES = ("group", "member")
+OVER_ROWS = (((0,), (0,)), ((), ()))
+OVER_FEATURES = (((1,), (1,)), ((), ()))
 
 
 def expert_block(
@@ -49,7 +53,7 @@
     return (slot_grad, slot_gate, gate_grad, up_grad, down_grad)
 
 
-def body(
+def pair_body(
     tokens,
     grad_out,
     expert_ids,
@@ -111,28 +115,107 @@
     )
 
 
+def dense_body(
+    tokens,
+    grad_out,
+    expert_ids,
+    pair_slot,
+    gate_weights,
+    weight_gate,
+    weight_up,
+    weight_down,
+    saved_gate,
+    saved_up,
+):
+    groups = lax.axis_size("group")
+    members = lax.axis_size("member")
+    experts = groups * members
+    me = lax.axis_index("group") * members + lax.axis_index("member")
+    tok_rows, width = tokens.shape
+    capacity = saved_gate.shape[1]
+    pair = capacity // experts
+    f32, bf16 = jnp.float32, jnp.bfloat16
+
+    all_grads = lax.all_gather(grad_out, AXES, axis=0, tiled=True)
+    meta = jnp.concatenate(
+        [expert_ids.astype(bf16), pair_slot.astype(bf16), gate_weights], axis=1
+    )
+    all_meta = lax.all_gather(meta, AXES, axis=0, tiled=True)
+    route = expert_ids.shape[1]
+    all_meta = all_meta.reshape(experts, tok_rows, 3, route).astype(f32)
+    mine = all_meta[:, :, 0] == me.astype(f32)
+    slot = jnp.sum(jnp.where(mine, all_meta[:, :, 1] + 1.0, 0.0), axis=2) - 1.0
+    gate = jnp.sum(jnp.where(mine, all_meta[:, :, 2], 0.0), axis=2)
+    pick = slot[:, None, :] == jnp.arange(pair, dtype=f32)[None, :, None]
+    route_scale = jnp.sum(jnp.where(pick, gate[:, None, :], 0.0), axis=2).reshape(capacity, 1)
+    pick = pick.astype(bf16)
+
+    def rows_of(x):
+        x = x.reshape(experts, tok_rows, width)
+        got = lax.dot_general(pick, x, (((2,), (1,)), ((0,), (0,))), preferred_element_type=f32)
+        return got.astype(bf16).reshape(capacity, width)
+
+    grad_rows = rows_of(all_grads)
+    all_tokens = lax.all_gather(tokens, AXES, axis=0, tiled=True)
+
+    a = saved_gate[0].astype(f32)
+    b = saved_up[0].astype(f32)
+    sig = jax.nn.sigmoid(a)
+    swish = a * sig
+    hidden = swish * b
+    back_hidden = lax.dot_general(
+        grad_rows, weight_down[0], OVER_FEATURES, preferred_element_type=f32
+    )
+    slot_gate = jnp.sum(hidden * back_hidden, axis=1).astype(bf16)
+    hidden_grad = route_scale * back_hidden
+    pregate = (hidden_grad * b * sig * (1.0 + a * (1.0 - sig))).astype(bf16)
+    preup = (hidden_grad * swish).astype(bf16)
+    slot_grad = (
+        lax.dot_general(pregate, weight_gate[0], OVER_FEATURES, preferred_element_type=f32)
+        + lax.dot_general(preup, weight_up[0], OVER_FEATURES, preferred_element_type=f32)
+    ).astype(bf16)
+    lanes = 128
+    lane = (jnp.arange(lanes) == me).astype(bf16)
+    tail = slot_gate[:, None] * lane[None, :]
+    send = jnp.concatenate([slot_grad, tail], axis=1).reshape(experts, pair, width + lanes)
+    dense = lax.dot_general(pick, send, (((1,), (1,)), ((0,), (0,))), preferred_element_type=f32)
+    dense = dense.astype(bf16).reshape(experts * tok_rows, width + lanes)
+    back = lax.psum_scatter(dense, AXES, scatter_dimension=0, tiled=True)
+
+    scaled = (route_scale * grad_rows.astype(f32)).astype(bf16)
+    down_grad = lax.dot_general(
+        hidden.astype(bf16), scaled, OVER_ROWS, preferred_element_type=f32
+    )
+    token_rows = rows_of(all_tokens)
+    gate_grad = lax.dot_general(token_rows, pregate, OVER_ROWS, preferred_element_type=f32)
+    up_grad = lax.dot_general(token_rows, preup, OVER_ROWS, preferred_element_type=f32)
+
+    grad_tokens = back[:, :width]
+    terms = back[:, width:].astype(f32)
+    hit = expert_ids[:, :, None] == jnp.arange(lanes, dtype=jnp.int32)[None, None, :]
+    grad_gates = jnp.sum(jnp.where(hit, terms[:, None, :], 0.0), axis=2).astype(bf16)
+    return (
+        grad_tokens,
+        grad_gates,
+        gate_grad.astype(bf16)[None],
+        up_grad.astype(bf16)[None],
+        down_grad.astype(bf16)[None],
+    )
+
+
+def body(*args):
+    devices = lax.axis_size("group") * lax.axis_size("member")
+    if devices * args[0].shape[0] <= 4 * args[8].shape[1]:
+        return dense_body(*args)
+    return pair_body(*args)
+
+
 def solution(mesh):
+    flat, deep = P(AXES, None), P(AXES, None, None)
     return jax.shard_map(
         body,
         mesh=mesh,
-        in_specs=(
-            P(("group", "member"), None),
-            P(("group", "member"), None),
-            P(("group", "member"), None),
-            P(("group", "member"), None),
-            P(("group", "member"), None),
-            P(("group", "member"), None, None),
-            P(("group", "member"), None, None),
-            P(("group", "member"), None, None),
-            P(("group", "member"), None, None),
-            P(("group", "member"), None, None),
-        ),
-        out_specs=(
-            P(("group", "member"), None),
-            P(("group", "member"), None),
-            P(("group", "member"), None, None),
-            P(("group", "member"), None, None),
-            P(("group", "member"), None, None),
-        ),
+        in_specs=(flat,) * 5 + (deep,) * 5,
+        out_specs=(flat, flat, deep, deep, deep),
         check_vma=False,
     )

time: 527 us -> 639 us (1.21)
  waiting for transfers between devices: 210 us -> 460 us
  blocking collectives: 143 us -> 63.7 us
  local copies, waits for them, and re-layouts: 70.7 us -> 12.4 us
  starting transfers between devices: 20.7 us -> 0.11 us
  matrix products: 59.7 us -> 78.8 us
  other arithmetic: 21.1 us -> 7.4 us
  between operations: 0.8 us -> 13.9 us
    reduce_scatter x0 -> x1, waiting for transfers between devices: none -> 354 us  [dense_body(): back = lax.psum_scatter(dense, AXES, scatter_dimension=0, tiled=True)]
    all_to_all x4 -> x0, waiting for transfers between devices: 210 us -> none  [the longest x1 108 us: body(): lax.all_to_all(send_rows, ('group', 'member'), split_axis=0, concat_axis=...]
    all_to_all x1 -> x0, blocking collectives: 143 us -> none  [body(): lax.all_to_all(send_grads, ('group', 'member'), split_axis=0, concat_axis...]
    all_gather x0 -> x2, waiting for transfers between devices: none -> 104 us  [the longest x1 60.6 us: dense_body(): all_tokens = lax.all_gather(tokens, AXES, axis=0, tiled=True)]
    all_gather x0 -> x1, blocking collectives: none -> 63.7 us  [dense_body(): all_meta = lax.all_gather(meta, AXES, axis=0, tiled=True)]
    gather x6 -> x0, local copies, waits for them, and re-layouts: 47.1 us -> none  [the longest x1 13.8 us: body(): send_rows = jnp.take(tokens, slot_token, axis=0, mode='fill', fill_value=0)]
    all_to_all x4 -> x0, starting transfers between devices: 20.7 us -> none  [the longest x1 6.32 us: body(): lax.all_to_all(send_gates, ('group', 'member'), split_axis=0, concat_axis...]
    dot_general x6 -> x9, matrix products: 59.7 us -> 78.8 us  [the longest x2 21.2 us: rows_of(): lax.dot_general(pick, x, (((2,), (1,)), ((0,), (0,))), preferred_element_...]
  transfers between devices with their start and end apart: 4 -> 3, of which waited for: 2 -> 3; matrix products, arithmetic and copies ran while one was open for 23% -> 15% of each run, Pallas kernels for 0% -> 0%
where the time goes in v1:
time: 639 us; the launch traced here: 636 us
  waiting for transfers between devices  460 us (72%)
  matrix products  78.8 us (12%)
  blocking collectives  63.7 us (10%)
  between operations  13.9 us (2%)
  local copies, waits for them, and re-layouts  12.4 us (2%)
  other arithmetic  7.4 us (1%)
    reduce_scatter x1, waiting for transfers between devices, dense_body(): back = lax.psum_scatter(dense, AXES, scatter_dimension=0, tiled=True)  354 us
    all_gather x1, blocking collectives, dense_body(): all_meta = lax.all_gather(meta, AXES, axis=0, tiled=True)  63.7 us
    all_gather x1, waiting for transfers between devices, dense_body(): all_tokens = lax.all_gather(tokens, AXES, axis=0, tiled=True)  60.6 us
    all_gather x1, waiting for transfers between devices, dense_body(): all_grads = lax.all_gather(grad_out, AXES, axis=0, tiled=True)  43.7 us
    dot_general x2, matrix products, rows_of(): lax.dot_general(pick, x, (((2,), (1,)), ((0,), (0,))), preferred_element_...  21.2 us
  transfers between devices with their start and end apart: 3, of which 3 were waited for; matrix products, arithmetic and copies ran while one was open for 15% of the time, Pallas kernels for 0%

profile of v1, /device:TPU:9, one launch (start us, length us, event | category | flops | bytes accessed | tf_op | source)
XLA Modules:
  0.0 636.5 jit_solution(14308835058858056274)
XLA Ops:
  7.2 0.0 copy-start
  7.2 0.0 all-gather.3.cloned.1.call-start
  7.2 0.7 all-gather.3.cloned.1.call-update
  7.9 0.0 all-gather.5.cloned.1.call-start
  8.0 0.7 all-gather.5.cloned.1.call-update
  8.7 0.0 reduce-scatter.2.cloned.1.call-start
  8.7 0.7 convert_element_type.98
  9.4 0.7 convert_element_type.97
  10.1 0.7 pad_maximum_fusion.1
  10.8 63.7 %all_gather.9 = bf16[4096,24]{0,1:T(8,128)(2,1)S(1)} all-gather(bf16[128,24]{0,1:T(8,128)(2,1)S(1)} %pad_maximum_fusion.1), channel_id=1, replica_groups=mesh['group'=8,'member'=4] {'group','member'}, dimensions={0}, use_global_device_ids=true | all-gather | bytes 202752 | tf_op jit(solution)/shard_map/all_gather | solution.py:143
  74.5 0.1 fusion.31
  74.6 0.3 select_reduce_fusion
  74.9 0.1 mul.66
  75.0 4.6 copy.19
  79.7 4.3 copy.18
  83.9 43.7 %all-gather.3.cloned.1.call-done = bf16[4096,2048]{1,0:T(8,128)(2,1)} async-done(((bf16[128,2048]{1,0:T(8,128)(2,1)}), bf16[4096,2048]{1,0:T(8,128)(2,1)}) %all-gather.3.cloned.1.call-update) | async-done | bytes 16777232 | tf_op jit(solution)/shard_map/all_gather | solution.py:139
  127.7 0.0 copy-start.2
  127.7 0.0 copy-start.4
  127.7 13.0 %multiply_convert_fusion = (bf16[32,48,2048]{2,1,0:T(8,128)(2,1)}, bf16[32,48,2048]{2,1,0:T(8,128)(2,1)}) fusion(f32[32,48]{1,0:T(8,128)S(1)} %select_reduce_fusion, bf16[32,128,2048]{2,1,0:T(8,128)(2,1)} %bitcast.84, f32[32,128]{1,0:T(8,128)S(1)} %broadcast_add_fusion), kind=kOutput, calls=%fused_computation.1 | convolution fusion | flops 818085888 | bytes 29382656 | tf_op jit(solution)/shard_map/dot_general | solution.py:155
  140.6 0.0 copy-done.2
  140.6 0.0 copy-done.4
  140.6 10.3 %fusion.7 = (bf16[1536,768]{0,1:T(8,128)(2,1)S(1)}, bf16[1536]{0:T(1024)(128)(2,1)S(1)}, bf16[1536,768]{0,1:T(8,128)(2,1)S(1)}) fusion(bf16[1,1536,768]{1,2,0:T(8,128)(2,1)S(1)} %copy-done.4, bf16[1,1536,768]{1,2,0:T(8,128)(2,1)S(1)} %copy-done.2, f32[1536]{0:T(1024)S(1)} %mul.66, bf16[1536,2048]{1,0:T(8,128)(2,1)} %bitcast.90, bf16[1,768,2048]{2,1,0:T(8,128)(2,1)} %param.17), kind=kOutput, calls=%fused_computation.16 | convolution fusion | flops 4854249984 | bytes 18883584 | tf_op jit(solution)/shard_map/dot_general | solution.py:166
  151.0 0.0 copy-start.8
  151.0 0.0 copy-start.10
  151.0 0.3 broadcast_multiply_fusion
  151.3 0.0 copy-done
  151.3 0.0 copy-start.7
  151.3 8.3 %fusion.19 = f32[1536,2048]{1,0:T(8,128)} fusion(bf16[1536,768]{0,1:T(8,128)(2,1)S(1)} %get-tuple-element.12, bf16[1,2048,768]{2,1,0:T(8,128)(2,1)S(1)} %copy-done), kind=kOutput, calls=%fused_computation.34 | convolution fusion | flops 4831838208 | bytes 18087936 | tf_op jit(solution)/shard_map/dot_general | solution.py:174
  159.6 0.0 copy-done.8
  159.6 0.0 copy-done.10
  159.6 0.0 copy-done.7
  159.6 10.2 %add_convert_fusion = bf16[1536,2048]{1,0:T(8,128)(2,1)} fusion(f32[1536,2048]{1,0:T(8,128)} %fusion.19, bf16[1536,768]{0,1:T(8,128)(2,1)S(1)} %get-tuple-element.14, bf16[1,2048,768]{2,1,0:T(8,128)(2,1)S(1)} %copy-done.7), kind=kOutput, calls=%fused_computation.2 | convolution fusion | flops 4838129664 | bytes 24379392 | tf_op jit(solution)/shard_map/dot_general | solution.py:175
  169.8 3.5 pad_maximum_fusion
  173.3 8.6 %convolution_convert_fusion = bf16[32,128,2176]{2,1,0:T(8,128)(2,1)} fusion(bf16[32,48,2176]{2,1,0:T(8,128)(2,1)S(1)} %bitcast.85, f32[32,128]{1,0:T(8,128)S(1)} %broadcast_add_fusion), kind=kOutput, calls=%fused_computation | convolution fusion | flops 864747520 | bytes 24526848 | tf_op jit(solution)/shard_map/dot_general | solution.py:181
  181.9 0.0 copy-start.6
  181.9 0.0 reduce-scatter.2.cloned.1.call-update
  181.9 0.7 copy-done.6
  182.6 0.1 copy.20
  182.7 60.6 %all-gather.5.cloned.1.call-done = bf16[4096,2048]{1,0:T(8,128)(2,1)} async-done(((bf16[128,2048]{1,0:T(8,128)(2,1)}), bf16[4096,2048]{1,0:T(8,128)(2,1)}) %all-gather.5.cloned.1.call-update) | async-done | bytes 16777232 | tf_op jit(solution)/shard_map/all_gather | solution.py:159
  243.3 0.0 copy-start.9
  243.3 8.2 %convolution_convert_fusion.1 = bf16[32,48,2048]{2,1,0:T(8,128)(2,1)S(1)} fusion(bf16[32,128,2048]{2,1,0:T(8,128)(2,1)} %bitcast.86, f32[32,128]{1,0:T(8,128)S(1)} %broadcast_add_fusion), kind=kOutput, calls=%fused_computation.28 | convolution fusion | flops 808648704 | bytes 23085056 | tf_op jit(solution)/shard_map/dot_general | solution.py:155
  251.5 0.0 copy-done.9
  251.5 0.0 copy-start.11
  251.5 0.0 slice-start
  251.5 6.5 %fusion.23 = bf16[1,2048,768]{2,1,0:T(8,128)(2,1)} fusion(bf16[1536,2048]{1,0:T(8,128)(2,1)S(1)} %bitcast.91, bf16[1536,768]{0,1:T(8,128)(2,1)S(1)} %copy-done.9), kind=kOutput, calls=%fused_computation.38 | convolution fusion | flops 4833411072 | bytes 11796480 | tf_op jit(solution)/shard_map/dot_general | solution.py:190
  258.1 0.0 copy-done.11
  258.1 0.0 slice-start.1
  258.1 0.0 copy-start.3
  258.1 0.0 copy-start.5
  258.1 6.5 %fusion.24 = bf16[1,2048,768]{2,1,0:T(8,128)(2,1)} fusion(bf16[1536,2048]{1,0:T(8,128)(2,1)S(1)} %bitcast.92, bf16[1536,768]{0,1:T(8,128)(2,1)S(1)} %copy-done.11), kind=kOutput, calls=%fused_computation.39 | convolution fusion | flops 4833411072 | bytes 11796480 | tf_op jit(solution)/shard_map/dot_general | solution.py:191
  264.6 0.0 slice-done
  264.6 0.0 slice-done.1
  264.6 0.0 copy-done.3
  264.6 0.0 copy-done.5
  264.6 0.0 copy-start.1
  264.6 7.1 %fusion.25 = bf16[1,768,2048]{2,1,0:T(8,128)(2,1)} fusion(bf16[1536,2048]{1,0:T(8,128)(2,1)S(1)} %bitcast.89, bf16[1,1536,768]{1,2,0:T(8,128)(2,1)S(1)} %copy-done.5, bf16[1,1536,768]{1,2,0:T(8,128)(2,1)S(1)} %copy-done.3), kind=kOutput, calls=%fused_computation.40 | convolution fusion | flops 4842848256 | bytes 14155776 | tf_op jit(solution)/shard_map/dot_general | solution.py:186
  271.8 354.5 %reduce-scatter.2.cloned.1.call-done = bf16[128,2176]{1,0:T(8,128)(2,1)} async-done(((bf16[4096,2176]{1,0:T(8,128)(2,1)}), bf16[128,2176]{1,0:T(8,128)(2,1)}) %reduce-scatter.2.cloned.1.call-update) | async-done | bytes 557072 | tf_op jit(solution)/shard_map/reduce_scatter | solution.py:183
  626.3 0.8 slice_convert_fusion
  627.0 0.4 select_reduce_fusion.1
  627.4 0.7 copy.21
  628.1 1.9 slice.23
  630.0 0.0 copy-done.1
  (4 shorter events, 0.0 us)
Async XLA Ops:
  7.2 144.1 %copy-start = (bf16[1,2048,768]{2,1,0:T(8,128)(2,1)S(1)}, bf16[1,2048,768]{2,1,0:T(8,128)(2,1)}, u32[]{:S(2)}) copy-start(bf16[1,2048,768]{2,1,0:T(8,128)(2,1)} %param.15) | copy-start | bytes 9437188
  7.2 120.5 %all-gather.3.cloned.1.call-start = ((), (), s32[]{:S(2)}) async-start(), calls=%async_computation.1 | async-start | bytes 17301504 | tf_op jit(solution)/shard_map/all_gather | solution.py:139
  7.9 235.4 %all-gather.5.cloned.1.call-start = ((), (), s32[]{:S(2)}) async-start(), calls=%async_computation.3 | async-start | bytes 17301504 | tf_op jit(solution)/shard_map/all_gather | solution.py:159
  8.7 617.6 %reduce-scatter.2.cloned.1.call-start = ((), (), s32[]{:S(2)}) async-start(), calls=%async_computation.2 | async-start | bytes 18382848 | tf_op jit(solution)/shard_map/reduce_scatter | solution.py:183
  127.7 13.0 %copy-start.2 = (bf16[1,1536,768]{1,2,0:T(8,128)(2,1)S(1)}, bf16[1,1536,768]{1,2,0:T(8,128)(2,1)}, u32[]{:S(2)}) copy-start(bf16[1,1536,768]{1,2,0:T(8,128)(2,1)} %copy.19) | copy-start | bytes 7077892
  127.7 13.0 %copy-start.4 = (bf16[1,1536,768]{1,2,0:T(8,128)(2,1)S(1)}, bf16[1,1536,768]{1,2,0:T(8,128)(2,1)}, u32[]{:S(2)}) copy-start(bf16[1,1536,768]{1,2,0:T(8,128)(2,1)} %copy.18) | copy-start | bytes 7077892
  151.0 8.6 %copy-start.8 = (bf16[1536,768]{0,1:T(8,128)(2,1)}, bf16[1536,768]{0,1:T(8,128)(2,1)S(1)}, u32[]{:S(2)}) copy-start(bf16[1536,768]{0,1:T(8,128)(2,1)S(1)} %get-tuple-element.12) | copy-start | bytes 7077892
  151.0 8.6 %copy-start.10 = (bf16[1536,768]{0,1:T(8,128)(2,1)}, bf16[1536,768]{0,1:T(8,128)(2,1)S(1)}, u32[]{:S(2)}) copy-start(bf16[1536,768]{0,1:T(8,128)(2,1)S(1)} %get-tuple-element.14) | copy-start | bytes 7077892
  151.3 8.3 %copy-start.7 = (bf16[1,2048,768]{2,1,0:T(8,128)(2,1)S(1)}, bf16[1,2048,768]{2,1,0:T(8,128)(2,1)}, u32[]{:S(2)}) copy-start(bf16[1,2048,768]{2,1,0:T(8,128)(2,1)} %param.16) | copy-start | bytes 9437188
  181.9 0.7 copy-start.6
  243.3 8.2 %copy-start.9 = (bf16[1536,768]{0,1:T(8,128)(2,1)S(1)}, bf16[1536,768]{0,1:T(8,128)(2,1)}, u32[]{:S(2)}) copy-start(bf16[1536,768]{0,1:T(8,128)(2,1)} %copy-done.8) | copy-start | bytes 7077892
  251.5 6.6 %copy-start.11 = (bf16[1536,768]{0,1:T(8,128)(2,1)S(1)}, bf16[1536,768]{0,1:T(8,128)(2,1)}, u32[]{:S(2)}) copy-start(bf16[1536,768]{0,1:T(8,128)(2,1)} %copy-done.10) | copy-start | bytes 7077892
  251.5 13.1 %slice-start = ((s8[6291456]{0:T(1024)(128)(4,1)}), s8[4194304]{0:T(1024)(128)(4,1)S(1)}, s32[]{:S(2)}) async-start(s8[6291456]{0:T(1024)(128)(4,1)} %bitcast.87), calls=%async_computation.4 | async-start | bytes 8388608
  258.1 6.5 %slice-start.1 = ((s8[6291456]{0:T(1024)(128)(4,1)}), s8[2097152]{0:T(1024)(128)(4,1)S(1)}, s32[]{:S(2)}) async-start(s8[6291456]{0:T(1024)(128)(4,1)} %bitcast.87), calls=%async_computation.5 | async-start | bytes 4194304
  258.1 6.5 %copy-start.3 = (bf16[1,1536,768]{1,2,0:T(8,128)(2,1)S(1)}, bf16[1,1536,768]{1,2,0:T(8,128)(2,1)}, u32[]{:S(2)}) copy-start(bf16[1,1536,768]{1,2,0:T(8,128)(2,1)} %copy.19) | copy-start | bytes 7077892
  258.1 6.5 %copy-start.5 = (bf16[1,1536,768]{1,2,0:T(8,128)(2,1)S(1)}, bf16[1,1536,768]{1,2,0:T(8,128)(2,1)}, u32[]{:S(2)}) copy-start(bf16[1,1536,768]{1,2,0:T(8,128)(2,1)} %copy.18) | copy-start | bytes 7077892
  264.6 365.3 %copy-start.1 = (bf16[1,2048,768]{2,1,0:T(8,128)(2,1)S(1)}, bf16[1,2048,768]{2,1,0:T(8,128)(2,1)}, u32[]{:S(2)}) copy-start(bf16[1,2048,768]{2,1,0:T(8,128)(2,1)} %param.15) | copy-start | bytes 9437188
Sparse Core Ops, SparseCore 0:
  11.0 116.6 all-gather.2
  130.6 112.5 all-gather.4
  245.6 380.6 reduce-scatter.1

commit v2 on v1

--- a/solution.py
+++ b/solution.py
@@ -174,13 +174,8 @@
         lax.dot_general(pregate, weight_gate[0], OVER_FEATURES, preferred_element_type=f32)
         + lax.dot_general(preup, weight_up[0], OVER_FEATURES, preferred_element_type=f32)
     ).astype(bf16)
-    lanes = 128
-    lane = (jnp.arange(lanes) == me).astype(bf16)
-    tail = slot_gate[:, None] * lane[None, :]
-    send = jnp.concatenate([slot_grad, tail], axis=1).reshape(experts, pair, width + lanes)
-    dense = lax.dot_general(pick, send, (((1,), (1,)), ((0,), (0,))), preferred_element_type=f32)
-    dense = dense.astype(bf16).reshape(experts * tok_rows, width + lanes)
-    back = lax.psum_scatter(dense, AXES, scatter_dimension=0, tiled=True)
+    back = lax.all_to_all(slot_grad, AXES, split_axis=0, concat_axis=0, tiled=True)
+    terms = lax.all_to_all(slot_gate, AXES, split_axis=0, concat_axis=0, tiled=True)
 
     scaled = (route_scale * grad_rows.astype(f32)).astype(bf16)
     down_grad = lax.dot_general(
@@ -190,10 +185,12 @@
     gate_grad = lax.dot_general(token_rows, pregate, OVER_ROWS, preferred_element_type=f32)
     up_grad = lax.dot_general(token_rows, preup, OVER_ROWS, preferred_element_type=f32)
 
-    grad_tokens = back[:, :width]
-    terms = back[:, width:].astype(f32)
-    hit = expert_ids[:, :, None] == jnp.arange(lanes, dtype=jnp.int32)[None, None, :]
-    grad_gates = jnp.sum(jnp.where(hit, terms[:, None, :], 0.0), axis=2).astype(bf16)
+    dest = expert_ids * pair + pair_slot
+    hit = dest[:, :, None] == jnp.arange(capacity, dtype=jnp.int32)[None, None, :]
+    grad_gates = jnp.sum(jnp.where(hit, terms.astype(f32), 0.0), axis=2).astype(bf16)
+    grad_tokens = lax.dot_general(
+        jnp.any(hit, axis=1).astype(bf16), back, (((1,), (0,)), ((), ())), preferred_element_type=f32
+    ).astype(bf16)
     return (
         grad_tokens,
         grad_gates,

time: 639 us -> 378 us (0.59)
  waiting for transfers between devices: 460 us -> 204 us
  starting transfers between devices: 0.11 us -> 9.88 us
  matrix products: 78.8 us -> 72.3 us
    reduce_scatter x1 -> x0, waiting for transfers between devices: 354 us -> none  [dense_body(): back = lax.psum_scatter(dense, AXES, scatter_dimension=0, tiled=True)]
    all_gather x1, waiting for transfers between devices: 60.6 us -> 134 us  [dense_body(): all_tokens = lax.all_gather(tokens, AXES, axis=0, tiled=True)]
    all_to_all x0 -> x2, waiting for transfers between devices: none -> 21.2 us  [the longest x1 21.2 us: dense_body(): lax.all_to_all(slot_grad, AXES, split_axis=0, concat_axis=0, tiled=True)]
    all_to_all x0 -> x2, starting transfers between devices: none -> 9.8 us  [the longest x1 5.89 us: dense_body(): lax.all_to_all(slot_grad, AXES, split_axis=0, concat_axis=0, tiled=True)]
  transfers between devices with their start and end apart: 3 -> 4, of which waited for: 3 -> 3; matrix products, arithmetic and copies ran while one was open for 15% -> 22% of each run, Pallas kernels for 0% -> 0%
where the time goes in v2:
time: 378 us; the launch traced here: 377 us
  waiting for transfers between devices  204 us (54%)
  matrix products  72.3 us (19%)
  blocking collectives  62.3 us (16%)
  between operations  14.3 us (4%)
  local copies, waits for them, and re-layouts  10.2 us (3%)
  starting transfers between devices  9.88 us (3%)
  other arithmetic  4.57 us (1%)
    all_gather x1, waiting for transfers between devices, dense_body(): all_tokens = lax.all_gather(tokens, AXES, axis=0, tiled=True)  134 us
    all_gather x1, blocking collectives, dense_body(): all_meta = lax.all_gather(meta, AXES, axis=0, tiled=True)  62.3 us
    all_gather x1, waiting for transfers between devices, dense_body(): all_grads = lax.all_gather(grad_out, AXES, axis=0, tiled=True)  47.4 us
    all_to_all x1, waiting for transfers between devices, dense_body(): lax.all_to_all(slot_grad, AXES, split_axis=0, concat_axis=0, tiled=True)  21.2 us
    dot_general x2, matrix products, rows_of(): lax.dot_general(pick, x, (((2,), (1,)), ((0,), (0,))), preferred_element_...  21.2 us
    dot_general x1, matrix products, dense_body(): lax.dot_general(grad_rows, weight_down[0], OVER_FEATURES, preferred_eleme...  11.7 us
    unnamed x33, local copies, waits for them, and re-layouts  9.29 us
  transfers between devices with their start and end apart: 4, of which 3 were waited for; matrix products, arithmetic and copies ran while one was open for 22% of the time, Pallas kernels for 0%

profile of v2, /device:TPU:9, one launch (start us, length us, event | category | flops | bytes accessed | tf_op | source)
XLA Modules:
  0.0 377.2 jit_solution(17915200260891188762)
XLA Ops:
  7.2 0.0 copy-start
  7.2 0.0 all-gather.3.cloned.1.call-start
  7.2 0.7 all-gather.3.cloned.1.call-update
  7.9 0.0 all-gather.5.cloned.1.call-start
  8.0 0.7 all-gather.5.cloned.1.call-update
  8.7 0.0 copy-start.6
  8.7 0.0 copy-start.7
  8.7 0.0 copy-start.8
  8.7 4.3 %copy.26 = bf16[1,1536,768]{1,2,0:T(8,128)(2,1)} copy(bf16[1,1536,768]{2,1,0:T(8,128)(2,1)} %param.19) | data formatting | bytes 4718592 | tf_op args[9]
  13.0 4.3 %copy.27 = bf16[1,1536,768]{1,2,0:T(8,128)(2,1)} copy(bf16[1,1536,768]{2,1,0:T(8,128)(2,1)} %param.18) | data formatting | bytes 4718592 | tf_op args[8]
  17.3 0.0 copy-done.6
  17.3 0.0 copy-done.7
  17.3 0.0 copy-done.8
  17.3 62.3 %all_gather.9 = bf16[4096,24]{0,1:T(8,128)(2,1)S(1)} all-gather(bf16[128,24]{0,1:T(8,128)(2,1)S(1)} %pad_maximum_fusion), channel_id=1, replica_groups=mesh['group'=8,'member'=4] {'group','member'}, dimensions={0}, use_global_device_ids=true | all-gather | bytes 202752 | tf_op jit(solution)/shard_map/all_gather | solution.py:143
  79.7 0.1 fusion.31
  79.8 0.3 select_reduce_fusion.1
  80.1 0.1 mul.61
  80.1 47.4 %all-gather.3.cloned.1.call-done = bf16[4096,2048]{1,0:T(8,128)(2,1)} async-done(((bf16[128,2048]{1,0:T(8,128)(2,1)}), bf16[4096,2048]{1,0:T(8,128)(2,1)}) %all-gather.3.cloned.1.call-update) | async-done | bytes 16777232 | tf_op jit(solution)/shard_map/all_gather | solution.py:139
  127.6 0.0 copy-start.2
  127.6 0.0 copy-start.4
  127.6 12.9 %multiply_convert_fusion = (bf16[32,48,2048]{2,1,0:T(8,128)(2,1)}, bf16[32,48,2048]{2,1,0:T(8,128)(2,1)}) fusion(f32[32,48]{1,0:T(8,128)S(1)} %select_reduce_fusion.1, bf16[32,128,2048]{2,1,0:T(8,128)(2,1)} %bitcast.84, f32[32,128]{1,0:T(8,128)S(1)} %broadcast_add_fusion), kind=kOutput, calls=%fused_computation | convolution fusion | flops 818085888 | bytes 29382656 | tf_op jit(solution)/shard_map/dot_general | solution.py:155
  140.5 0.0 copy-done.2
  140.5 0.0 copy-done.4
  140.5 11.7 %fusion.10 = (bf16[1536]{0:T(1024)(128)(2,1)S(1)}, bf16[1536,768]{0,1:T(8,128)(2,1)}, bf16[1536,768]{0,1:T(8,128)(2,1)}) fusion(bf16[1,1536,768]{1,2,0:T(8,128)(2,1)S(1)} %copy-done.2, bf16[1,1536,768]{1,2,0:T(8,128)(2,1)S(1)} %copy-done.4, f32[1536]{0:T(1024)S(1)} %mul.61, bf16[1536,2048]{1,0:T(8,128)(2,1)} %bitcast.89, bf16[1,768,2048]{2,1,0:T(8,128)(2,1)} %param.17), kind=kOutput, calls=%fused_computation.19 | convolution fusion | flops 4854249984 | bytes 18883584 | tf_op jit(solution)/shard_map/dot_general | solution.py:166
  152.2 0.7 convert_element_type.134
  152.9 3.9 %all-to-all-start.1 = ((bf16[32,48,1]{1,2,0:T(2,128)(2,1)}), bf16[32,48,1]{1,2,0:T(2,128)(2,1)S(1)}, u32[]{:S(2)}, u32[]{:S(2)}) async-start(bf16[32,48,1]{1,2,0:T(2,128)(2,1)} %convert_element_type.134), calls=%async_computation.1 | async-start | bytes 32768 | tf_op jit(solution)/shard_map/all_to_all | solution.py:178
  156.8 0.0 copy-done
  156.8 0.0 copy-start.9
  156.9 0.0 copy-start.11
  156.9 7.1 %fusion.20 = f32[1536,2048]{1,0:T(8,128)S(1)} fusion(bf16[1536,768]{0,1:T(8,128)(2,1)} %get-tuple-element.13, bf16[1,2048,768]{2,1,0:T(8,128)(2,1)S(1)} %copy-done), kind=kOutput, calls=%fused_computation.35 | convolution fusion | flops 4831838208 | bytes 18087936 | tf_op jit(solution)/shard_map/dot_general | solution.py:174
  164.0 0.0 copy-done.9
  164.0 0.0 copy-done.11
  164.0 7.5 %add_convert_fusion = bf16[1536,2048]{1,0:T(8,128)(2,1)} fusion(f32[1536,2048]{1,0:T(8,128)S(1)} %fusion.20, bf16[1536,768]{0,1:T(8,128)(2,1)S(1)} %copy-done.11, bf16[1,2048,768]{2,1,0:T(8,128)(2,1)S(1)} %copy-done.9), kind=kOutput, calls=%fused_computation.1 | convolution fusion | flops 4838129664 | bytes 24379392 | tf_op jit(solution)/shard_map/dot_general | solution.py:175
  171.5 0.0 all-to-all-done.1
  171.5 5.9 %all-to-all-start = ((bf16[32,48,2048]{2,1,0:T(8,128)(2,1)}), bf16[32,48,2048]{2,1,0:T(8,128)(2,1)}, u32[]{:S(2)}, u32[]{:S(2)}) async-start(bf16[32,48,2048]{2,1,0:T(8,128)(2,1)} %bitcast.92), calls=%async_computation | async-start | bytes 12582912 | tf_op jit(solution)/shard_map/all_to_all | solution.py:177
  177.4 0.1 copy.25
  177.5 3.1 fusion.3
  180.7 133.7 %all-gather.5.cloned.1.call-done = bf16[4096,2048]{1,0:T(8,128)(2,1)} async-done(((bf16[128,2048]{1,0:T(8,128)(2,1)}), bf16[4096,2048]{1,0:T(8,128)(2,1)}) %all-gather.5.cloned.1.call-update) | async-done | bytes 16777232 | tf_op jit(solution)/shard_map/all_gather | solution.py:159
  314.4 0.0 copy-start.10
  314.4 8.2 %convolution_convert_fusion = bf16[32,48,2048]{2,1,0:T(8,128)(2,1)S(1)} fusion(bf16[32,128,2048]{2,1,0:T(8,128)(2,1)} %bitcast.85, f32[32,128]{1,0:T(8,128)S(1)} %broadcast_add_fusion), kind=kOutput, calls=%fused_computation.29 | convolution fusion | flops 808648704 | bytes 23085056 | tf_op jit(solution)/shard_map/dot_general | solution.py:155
  322.6 0.0 copy-done.10
  322.6 0.0 copy-start.12
  322.6 0.0 slice-start
  322.6 6.5 %fusion.24 = bf16[1,2048,768]{2,1,0:T(8,128)(2,1)} fusion(bf16[1536,2048]{1,0:T(8,128)(2,1)S(1)} %bitcast.90, bf16[1536,768]{0,1:T(8,128)(2,1)S(1)} %copy-done.10), kind=kOutput, calls=%fused_computation.39 | convolution fusion | flops 4833411072 | bytes 11796480 | tf_op jit(solution)/shard_map/dot_general | solution.py:185
  329.2 0.0 copy-done.12
  329.2 0.0 slice-start.1
  329.2 0.0 copy-start.3
  329.2 0.0 copy-start.5
  329.2 6.5 %fusion.25 = bf16[1,2048,768]{2,1,0:T(8,128)(2,1)} fusion(bf16[1536,2048]{1,0:T(8,128)(2,1)S(1)} %bitcast.91, bf16[1536,768]{0,1:T(8,128)(2,1)S(1)} %copy-done.12), kind=kOutput, calls=%fused_computation.40 | convolution fusion | flops 4833411072 | bytes 11796480 | tf_op jit(solution)/shard_map/dot_general | solution.py:186
  335.7 0.0 slice-done
  335.7 0.0 slice-done.1
  335.7 0.0 copy-done.3
  335.7 0.0 copy-done.5
  335.7 0.0 copy-start.1
  335.7 7.2 %fusion.26 = bf16[1,768,2048]{2,1,0:T(8,128)(2,1)} fusion(bf16[1536,2048]{1,0:T(8,128)(2,1)S(1)} %bitcast.88, bf16[1,1536,768]{1,2,0:T(8,128)(2,1)S(1)} %copy-done.3, bf16[1,1536,768]{1,2,0:T(8,128)(2,1)S(1)} %copy-done.5), kind=kOutput, calls=%fused_computation.41 | convolution fusion | flops 4842848256 | bytes 14155776 | tf_op jit(solution)/shard_map/dot_general | solution.py:181
  342.9 0.1 convert_reduce_fusion
  343.0 0.1 reshape.75
  343.0 1.0 select_reduce_fusion
  344.0 0.7 copy.29
  344.7 21.2 %all-to-all-done = bf16[32,48,2048]{2,1,0:T(8,128)(2,1)} async-done(((bf16[32,48,2048]{2,1,0:T(8,128)(2,1)}), bf16[32,48,2048]{2,1,0:T(8,128)(2,1)}, u32[]{:S(2)}, u32[]{:S(2)}) %all-to-all-start) | async-done | bytes 6291488 | tf_op jit(solution)/shard_map/all_to_all | solution.py:177
  365.8 4.6 %convolution_convert_fusion.5 = bf16[128,2048]{1,0:T(8,128)(2,1)} fusion(pred[128,1536]{1,0:T(8,128)(4,1)S(1)} %fusion.3, bf16[1536,2048]{1,0:T(8,128)(2,1)} %bitcast.10), kind=kOutput, calls=%fused_computation.42 | convolution fusion | flops 805568512 | bytes 7012352 | tf_op jit(solution)/shard_map/dot_general | solution.py:191
  370.4 0.0 copy-done.1
  (5 shorter events, 0.0 us)
Async XLA Ops:
  7.2 149.7 %copy-start = (bf16[1,2048,768]{2,1,0:T(8,128)(2,1)S(1)}, bf16[1,2048,768]{2,1,0:T(8,128)(2,1)}, u32[]{:S(2)}) copy-start(bf16[1,2048,768]{2,1,0:T(8,128)(2,1)} %param.15) | copy-start | bytes 9437188
  7.2 120.4 %all-gather.3.cloned.1.call-start = ((), (), s32[]{:S(2)}) async-start(), calls=%async_computation.2 | async-start | bytes 17301504 | tf_op jit(solution)/shard_map/all_gather | solution.py:139
  7.9 306.4 %all-gather.5.cloned.1.call-start = ((), (), s32[]{:S(2)}) async-start(), calls=%async_computation.3 | async-start | bytes 17301504 | tf_op jit(solution)/shard_map/all_gather | solution.py:159
  8.7 8.6 %copy-start.6 = (s32[128,8]{0,1:T(8,128)S(1)}, s32[128,8]{0,1:T(8,128)}, u32[]{:S(2)}) copy-start(s32[128,8]{0,1:T(8,128)} %param.12) | copy-start | bytes 12292
  8.7 8.6 %copy-start.7 = (s32[128,8]{0,1:T(8,128)S(1)}, s32[128,8]{0,1:T(8,128)}, u32[]{:S(2)}) copy-start(s32[128,8]{0,1:T(8,128)} %param.13) | copy-start | bytes 12292
  8.7 8.6 %copy-start.8 = (bf16[128,8]{0,1:T(8,128)(2,1)S(1)}, bf16[128,8]{0,1:T(8,128)(2,1)}, u32[]{:S(2)}) copy-start(bf16[128,8]{0,1:T(8,128)(2,1)} %param.14) | copy-start | bytes 6148
  127.6 12.9 %copy-start.2 = (bf16[1,1536,768]{1,2,0:T(8,128)(2,1)S(1)}, bf16[1,1536,768]{1,2,0:T(8,128)(2,1)}, u32[]{:S(2)}) copy-start(bf16[1,1536,768]{1,2,0:T(8,128)(2,1)} %copy.26) | copy-start | bytes 7077892
  127.6 12.9 %copy-start.4 = (bf16[1,1536,768]{1,2,0:T(8,128)(2,1)S(1)}, bf16[1,1536,768]{1,2,0:T(8,128)(2,1)}, u32[]{:S(2)}) copy-start(bf16[1,1536,768]{1,2,0:T(8,128)(2,1)} %copy.27) | copy-start | bytes 7077892
  152.9 18.6 %all-to-all-start.1 = ((bf16[32,48,1]{1,2,0:T(2,128)(2,1)}), bf16[32,48,1]{1,2,0:T(2,128)(2,1)S(1)}, u32[]{:S(2)}, u32[]{:S(2)}) async-start(bf16[32,48,1]{1,2,0:T(2,128)(2,1)} %convert_element_type.134), calls=%async_computation.1 | async-start | bytes 32768 | tf_op jit(solution)/shard_map/all_to_all | solution.py:178
  156.8 7.1 %copy-start.9 = (bf16[1,2048,768]{2,1,0:T(8,128)(2,1)S(1)}, bf16[1,2048,768]{2,1,0:T(8,128)(2,1)}, u32[]{:S(2)}) copy-start(bf16[1,2048,768]{2,1,0:T(8,128)(2,1)} %param.16) | copy-start | bytes 9437188
  156.9 7.1 %copy-start.11 = (bf16[1536,768]{0,1:T(8,128)(2,1)S(1)}, bf16[1536,768]{0,1:T(8,128)(2,1)}, u32[]{:S(2)}) copy-start(bf16[1536,768]{0,1:T(8,128)(2,1)} %get-tuple-element.14) | copy-start | bytes 7077892
  171.5 194.3 %all-to-all-start = ((bf16[32,48,2048]{2,1,0:T(8,128)(2,1)}), bf16[32,48,2048]{2,1,0:T(8,128)(2,1)}, u32[]{:S(2)}, u32[]{:S(2)}) async-start(bf16[32,48,2048]{2,1,0:T(8,128)(2,1)} %bitcast.92), calls=%async_computation | async-start | bytes 12582912 | tf_op jit(solution)/shard_map/all_to_all | solution.py:177
  314.4 8.2 %copy-start.10 = (bf16[1536,768]{0,1:T(8,128)(2,1)S(1)}, bf16[1536,768]{0,1:T(8,128)(2,1)}, u32[]{:S(2)}) copy-start(bf16[1536,768]{0,1:T(8,128)(2,1)} %get-tuple-element.13) | copy-start | bytes 7077892
  322.6 6.6 %copy-start.12 = (bf16[1536,768]{0,1:T(8,128)(2,1)S(1)}, bf16[1536,768]{0,1:T(8,128)(2,1)}, u32[]{:S(2)}) copy-start(bf16[1536,768]{0,1:T(8,128)(2,1)} %get-tuple-element.14) | copy-start | bytes 7077892
  322.6 13.1 %slice-start = ((s8[6291456]{0:T(1024)(128)(4,1)}), s8[4194304]{0:T(1024)(128)(4,1)S(1)}, s32[]{:S(2)}) async-start(s8[6291456]{0:T(1024)(128)(4,1)} %bitcast.86), calls=%async_computation.4 | async-start | bytes 8388608
  329.2 6.5 %slice-start.1 = ((s8[6291456]{0:T(1024)(128)(4,1)}), s8[2097152]{0:T(1024)(128)(4,1)S(1)}, s32[]{:S(2)}) async-start(s8[6291456]{0:T(1024)(128)(4,1)} %bitcast.86), calls=%async_computation.5 | async-start | bytes 4194304
  329.2 6.5 %copy-start.3 = (bf16[1,1536,768]{1,2,0:T(8,128)(2,1)S(1)}, bf16[1,1536,768]{1,2,0:T(8,128)(2,1)}, u32[]{:S(2)}) copy-start(bf16[1,1536,768]{1,2,0:T(8,128)(2,1)} %copy.26) | copy-start | bytes 7077892
  329.2 6.5 %copy-start.5 = (bf16[1,1536,768]{1,2,0:T(8,128)(2,1)S(1)}, bf16[1,1536,768]{1,2,0:T(8,128)(2,1)}, u32[]{:S(2)}) copy-start(bf16[1,1536,768]{1,2,0:T(8,128)(2,1)} %copy.27) | copy-start | bytes 7077892
  335.7 34.7 %copy-start.1 = (bf16[1,2048,768]{2,1,0:T(8,128)(2,1)S(1)}, bf16[1,2048,768]{2,1,0:T(8,128)(2,1)}, u32[]{:S(2)}) copy-start(bf16[1,2048,768]{2,1,0:T(8,128)(2,1)} %param.15) | copy-start | bytes 9437188
Sparse Core Ops, SparseCore 0:
  11.0 116.5 all-gather.2
  130.6 183.7 all-gather.4
